TPU v7x, 32 devices: a whole 2x2x4 slice. The times are simulated.
32 devices in a mesh: old: 4 (over y, core), new: 8 (over z, x).
Axes of the slice: x: 2, y: 2, z: 4, core: 2. Of those that a mesh axis runs over, the one named last changes fastest.
Arguments:
- old_field: bfloat16 [3, 27, 98304], P(None, None, ('old', 'new')), may hold values from -6 to 6
- pair_dest: int32 [32768, 1], P(('old', 'new')), may hold values from 0 to 31; in each aligned block of 1024 rows (0 to 1023, 1024 to 2047, ...) at most 128 rows name the same one
- pair_new: int32 [32768], P(('old', 'new')), may hold values from 0 to 511
- pair_old: int32 [32768], P(('old', 'new')), may hold values from 0 to 3071
- pair_block: int32 [32768], P(('old', 'new')), may hold values from 0 to 3
- basis_old: bfloat16 [4, 27, 125], replicated, may hold values from -1.25 to 1.25
- basis_new: bfloat16 [4, 27, 125], replicated, may hold values from -0.5 to 0.5
- volume: float32 [2, 8, 1024], P(None, 'old', 'new'), may hold values from 0.25 to 36, as said below
Outputs:
- solution: float32 [3, 5, 16, 2048], P(None, None, 'old', 'new')
- residual: float32 [3, 5, 16, 2048], P(None, None, 'old', 'new')
Inputs may be any that keep to these rules, and one draw needn't show every extreme that they name: `pair_dest`: a device's index is its position along old times the number of devices along new plus its position along new; in each device's block of 1024 pairs at most 128 name one destination. `pair_new`: local element number (x * 2 + y) * 128 + z within the destination's block. `pair_old`: old element within the block of the device that holds the pair. `volume`: positive element factors.
All inputs are finite; a program needn't handle non-finite values.
Results may differ from a plain program's by a relative error of at most 0.003.
Values may be sent and summed in bfloat16 or wider, within the bound.
A program may use at most 64 MiB of HBM per device.

v0:
```python
import jax
import jax.numpy as jnp
import numpy as np
from jax import lax
from jax.sharding import PartitionSpec as P

ITERS = 4
LINE_MASS = np.array([[4.0, 2.0, -1.0], [2.0, 16.0, 2.0], [-1.0, 2.0, 4.0]]) / 15.0


def passed_along(shard, axis, by):
    size = lax.axis_size(axis)
    return lax.ppermute(shard, axis, [(i, (i + by) % size) for i in range(size)])


def split_axis(array, axis, count):
    moved = jnp.moveaxis(array, axis, -1)
    paired = moved[..., : 2 * count].reshape(moved.shape[:-1] + (count, 2))
    even_nodes = paired[..., 0]
    odd_nodes = paired[..., 1]
    after_nodes = jnp.concatenate(
        [even_nodes[..., 1:], moved[..., 2 * count : 2 * count + 1]], axis=-1
    )
    stacked = jnp.stack([even_nodes, odd_nodes, after_nodes], axis=0)
    return jnp.moveaxis(stacked, -1, axis + 1)


def pick_nodes(extended, cell_counts):
    along_first, along_second, along_third = cell_counts
    stacked = split_axis(extended, 3, along_third)
    stacked = split_axis(stacked, 3, along_second)
    stacked = split_axis(stacked, 3, along_first)
    return jnp.transpose(stacked, (3, 0, 1, 2, 4, 5, 6))


def merge_axis(array, local_axis, cell_axis):
    moved = jnp.moveaxis(array, (local_axis, cell_axis), (0, -1))
    count = moved.shape[-1]
    zero_pad = [(0, 0)] * (moved.ndim - 2)
    even_full = jnp.pad(moved[0], zero_pad + [(0, 1)]) + jnp.pad(moved[2], zero_pad + [(1, 0)])
    woven = jnp.stack([even_full[..., :count], moved[1]], axis=-1)
    woven = woven.reshape(woven.shape[:-2] + (2 * count,))
    return jnp.concatenate([woven, even_full[..., count:]], axis=-1)


def spread_nodes(element_nodes):
    summed = merge_axis(element_nodes, 3, 6)
    summed = merge_axis(summed, 2, 4)
    summed = merge_axis(summed, 1, 2)
    return jnp.transpose(summed, (0, 3, 2, 1))


def element_mass(element_nodes, volume):
    line_mass = jnp.asarray(LINE_MASS, dtype=jnp.float32)
    high = lax.Precision.HIGHEST
    applied = jnp.einsum("ia,cabdxyz->cibdxyz", line_mass, element_nodes, precision=high)
    applied = jnp.einsum("jb,cibdxyz->cijdxyz", line_mass, applied, precision=high)
    applied = jnp.einsum("kd,cijdxyz->cijkxyz", line_mass, applied, precision=high)
    return applied * volume


def fold_rims(assembled):
    front_face = passed_along(assembled[..., -1], "new", 1)
    inner_part = assembled[..., :-1]
    inner_part = jnp.concatenate(
        [inner_part[..., :1] + front_face[..., None], inner_part[..., 1:]], axis=3
    )
    side_face = passed_along(inner_part[:, :, -1, :], "old", 1)
    folded = inner_part[:, :, :-1]
    folded = jnp.concatenate(
        [folded[:, :, :1] + side_face[:, :, None, :], folded[:, :, 1:]], axis=2
    )
    return folded


def operate(vector, volume):
    upper_layer = passed_along(vector[..., 0], "new", -1)
    extended = jnp.concatenate([vector, upper_layer[..., None]], axis=3)
    upper_row = passed_along(extended[:, :, 0, :], "old", -1)
    extended = jnp.concatenate([extended, upper_row[:, :, None, :]], axis=2)
    element_nodes = pick_nodes(extended, volume.shape)
    return fold_rims(spread_nodes(element_mass(element_nodes, volume)))


def quadrature(coefficients, block_kind, basis_old, basis_new):
    summed = jnp.zeros(coefficients.shape, jnp.float32)
    for q in range(basis_old.shape[0]):
        chosen = jnp.where(
            (block_kind == q)[None, None, :], coefficients, jnp.zeros((), coefficients.dtype)
        )
        values = jnp.einsum(
            "cap,ak->ckp", chosen, basis_old[q], preferred_element_type=jnp.float32
        ).astype(jnp.bfloat16)
        summed = summed + jnp.einsum(
            "ckp,ak->cap", values, basis_new[q], preferred_element_type=jnp.float32
        )
    return summed


def squares(residual):
    return lax.psum(jnp.sum(residual * residual, axis=(1, 2, 3)), ("old", "new"))


def on_device(old_field, pair_dest, pair_new, pair_old, pair_block, basis_old, basis_new, volume):
    devices = lax.axis_size(("old", "new"))
    pair_count = pair_dest.shape[0]
    capacity = 4 * pair_count // devices
    cells_one, cells_two, cells_three = volume.shape
    elements = cells_one * cells_two * cells_three
    destination = pair_dest[:, 0]
    onehot = (destination[:, None] == jnp.arange(devices, dtype=jnp.int32)[None, :]).astype(
        jnp.int32
    )
    slot_rank = jnp.sum((jnp.cumsum(onehot, axis=0) - onehot) * onehot, axis=1)
    position = destination * capacity + slot_rank
    gathered = jnp.take(old_field, pair_old, axis=2)
    contribution = quadrature(gathered, pair_block, basis_old, basis_new)
    outgoing = (
        jnp.zeros((81, devices * capacity), jnp.float32)
        .at[:, position]
        .set(contribution.reshape(81, -1))
    )
    targets = jnp.full((devices * capacity,), elements, jnp.int32).at[position].set(pair_new)
    received, slot_element = (
        lax.all_to_all(
            outgoing.reshape(81, devices, capacity),
            ("old", "new"),
            split_axis=1,
            concat_axis=1,
            tiled=True,
        ),
        lax.all_to_all(
            targets.reshape(1, devices, capacity),
            ("old", "new"),
            split_axis=1,
            concat_axis=1,
            tiled=True,
        ),
    )
    arrived = received.reshape(81, -1)
    slot_element = slot_element.reshape(-1)
    element_load = (
        jnp.zeros((81, elements + 1), jnp.float32).at[:, slot_element].add(arrived)[:, :elements]
    )
    load_vector = fold_rims(
        spread_nodes(element_load.reshape(3, 3, 3, 3, cells_one, cells_two, cells_three))
    )
    solution = jnp.zeros_like(load_vector)
    residual = load_vector
    direction = load_vector
    norm_now = squares(residual)
    for iteration in range(ITERS):
        applied = operate(direction, volume)
        curvature = lax.psum(jnp.sum(direction * applied, axis=(1, 2, 3)), ("old", "new"))
        step_size = norm_now / curvature
        solution = solution + step_size[:, None, None, None] * direction
        residual = residual - step_size[:, None, None, None] * applied
        norm_next = squares(residual)
        direction = residual + (norm_next / norm_now)[:, None, None, None] * direction
        norm_now = norm_next
    return (solution, residual)


def solution(mesh):
    in_specs = (
        P(None, None, ("old", "new")),
        P(("old", "new"), None),
        P(("old", "new")),
        P(("old", "new")),
        P(("old", "new")),
        P(),
        P(),
        P(None, "old", "new"),
    )
    out_specs = (P(None, None, "old", "new"), P(None, None, "old", "new"))
    return jax.shard_map(
        on_device, mesh=mesh, in_specs=in_specs, out_specs=out_specs, check_vma=False
    )
```

profile of v0, /device:TPU:10, one launch (start us, length us, event | category | flops | bytes accessed | tf_op | source)
XLA Modules:
  0.0 578.3 jit_solution(5909297454449030575)
XLA Ops:
  1.3 9.0 %reduce-window.6 = s32[32,8,128]{2,1,0:T(8,128)S(1)} reduce-window(s32[32,8,128]{2,1,0:T(8,128)S(1)} %fusion.60, s32[]{:T(128)} %constant.17.clone.1), window={size=1x1x128 pad=0_0x0_0x127_0}, to_apply=%region_0.0 | reduce-window | flops 4161536 | bytes 262148 | tf_op jit(solution)/shard_map/reduce-window
  10.8 0.7 fusion.59
  12.3 5.1 scatter_custom_fusion
  17.3 6.0 %all-to-all-start = ((s32[1,32,128]{2,0,1:T(1,128)}), s32[1,32,128]{2,0,1:T(1,128)S(1)}, u32[]{:S(2)}, u32[]{:S(2)}) async-start(s32[1,32,128]{2,0,1:T(1,128)} %bitcast.6), calls=%async_computation | async-start | bytes 32768 | tf_op jit(solution)/shard_map/all_to_all | solution.py:132
  24.0 0.7 broadcast_compare_fusion.3
  24.8 4.5 copy.623
  30.0 7.5 %gather_fusion = bf16[1024,3,27]{2,1,0:T(4,128)(2,1)} fusion(bf16[3,27,3072]{1,0,2:T(4,128)(2,1)S(1)} %copy.623, s32[1024]{0:T(1024)S(1)} %fusion.106), kind=kCustom, calls=%fused_computation | custom fusion | bytes 335872 | tf_op jit(solution)/shard_map/jit(_take)/gather | solution.py:116
  37.6 9.2 %select_bitcast_fusion.3 = (bf16[3,27,1024]{1,0,2:T(4,128)(2,1)}, bf16[3,27,1024]{1,0,2:T(4,128)(2,1)S(1)}, bf16[3,27,1024]{1,0,2:T(4,128)(2,1)S(1)}, bf16[3,27,1024]{1,0,2:T(4,128)(2,1)S(1)}) fusion(pred[1024]{0:T(1024)(128)(4,1)S(1)} %get-tuple-element.120, bf16[1024,3,27]{2,1,0:T(4,128)(2,1)} %gather_fusion, pred[1024]{0:T(1024)(128)(4,1)S(1)} %get-tuple-element.126, ...), kind=kLoop, calls=%fused_computation.31 | loop fusion | flops 414720 | bytes 834560 | tf_op jit(solution)/shard_map/jit(_where)/select_n | solution.py:88
  46.8 1.4 fusion.6
  48.2 2.3 fusion.5
  50.4 1.4 fusion.4
  51.8 1.7 fusion.11
  53.8 3.8 scatter_custom_fusion.1
  57.6 1.8 copy.641
  59.3 5.8 %all-to-all-start.1 = ((f32[81,32,128]{2,0,1:T(8,128)}), f32[81,32,128]{2,0,1:T(8,128)S(1)}, u32[]{:S(2)}, u32[]{:S(2)}) async-start(f32[81,32,128]{2,0,1:T(8,128)} %copy.641), calls=%async_computation.1 | async-start | bytes 2883584 | tf_op jit(solution)/shard_map/all_to_all | solution.py:125
  65.8 31.4 %all-to-all-done.1 = f32[81,32,128]{2,0,1:T(8,128)S(1)} async-done(((f32[81,32,128]{2,0,1:T(8,128)}), f32[81,32,128]{2,0,1:T(8,128)S(1)}, u32[]{:S(2)}, u32[]{:S(2)}) %all-to-all-start.1) | async-done | bytes 1327136 | tf_op jit(solution)/shard_map/all_to_all | solution.py:125
  97.6 1.0 copy.830
  98.6 0.8 copy.643
  99.4 28.0 %scatter_custom_fusion.2 = f32[81,513]{0,1:T(8,128)S(1)} fusion(s32[4096]{0:T(1024)} %bitcast.616, f32[4096,81]{1,0:T(8,128)S(1)} %copy.643, f32[]{:T(128)} %constant.14.clone.1), kind=kCustom, calls=%fused_computation.113 | custom fusion | flops 331776 | bytes 166724 | tf_op jit(solution)/shard_map/scatter-add | solution.py:143
  128.1 4.3 copy.777
  132.4 6.2 %reshape.241 = f32[3,3,3,2,2,256]{5,4,3,0,1,2:T(2,128)S(1)} reshape(f32[3,3,3,2,2,128,2]{6,5,4,3,0,1,2:T(8,128)} %copy.777) | data formatting | bytes 221184 | tf_op jit(solution)/shard_map/reshape | solution.py:42
  140.1 3.0 collective-permute-done
  143.7 3.0 collective-permute-done.1
  147.0 2.4 collective-permute-start.2
  149.4 2.1 collective-permute-done.2
  151.8 1.6 collective-permute-done.3
  154.1 2.5 fusion.118
  156.6 2.2 copy.806
  162.4 4.3 copy.779
  166.7 6.2 %reshape.242 = f32[3,3,3,2,2,256]{5,4,3,0,1,2:T(2,128)S(1)} reshape(f32[3,3,3,2,2,128,2]{6,5,4,3,0,1,2:T(8,128)} %copy.779) | data formatting | bytes 221184 | tf_op jit(solution)/shard_map/reshape | solution.py:42
  174.5 3.0 collective-permute-done.4
  178.1 2.9 collective-permute-done.5
  181.4 45.8 %all-reduce.30 = (f32[3]{0:T(128)S(1)}, f32[3]{0:T(128)S(1)}) all-reduce(f32[3]{0:T(128)S(1)} %get-tuple-element.7, f32[3]{0:T(128)S(1)} %get-tuple-element.6), channel_id=1, replica_groups=mesh['old'=4,'new'=8] {'old','new'}, use_global_device_ids=true, to_apply=%region_7.8 | all-reduce | flops 6 | bytes 48 | tf_op jit(solution)/shard_map/psum | solution.py:101
  227.4 38.4 %psum.58 = f32[3]{0:T(128)S(1)} all-reduce(f32[3]{0:T(128)S(1)} %get-tuple-element.20), channel_id=1, replica_groups=mesh['old'=4,'new'=8] {'old','new'}, use_global_device_ids=true, to_apply=%region_11.12 | all-reduce | flops 3 | bytes 24 | tf_op jit(solution)/shard_map/psum | solution.py:101
  266.2 4.5 collective-permute-done.6
  271.2 1.6 collective-permute-done.7
  273.4 2.5 fusion.117
  275.9 2.2 copy.812
  281.7 4.3 copy.781
  286.0 6.2 %reshape.243 = f32[3,3,3,2,2,256]{5,4,3,0,1,2:T(2,128)S(1)} reshape(f32[3,3,3,2,2,128,2]{6,5,4,3,0,1,2:T(8,128)} %copy.781) | data formatting | bytes 221184 | tf_op jit(solution)/shard_map/reshape | solution.py:42
  293.2 3.6 collective-permute-done.8
  297.5 2.8 collective-permute-done.9
  300.6 42.8 %psum.59 = f32[3]{0:T(128)S(1)} all-reduce(f32[3]{0:T(128)S(1)} %get-tuple-element.18), channel_id=1, replica_groups=mesh['old'=4,'new'=8] {'old','new'}, use_global_device_ids=true, to_apply=%region_13.14 | all-reduce | flops 3 | bytes 24 | tf_op jit(solution)/shard_map/psum | solution.py:154
  343.6 39.3 %psum.60 = f32[3]{0:T(128)S(1)} all-reduce(f32[3]{0:T(128)S(1)} %get-tuple-element.16), channel_id=1, replica_groups=mesh['old'=4,'new'=8] {'old','new'}, use_global_device_ids=true, to_apply=%region_15.16 | all-reduce | flops 3 | bytes 24 | tf_op jit(solution)/shard_map/psum | solution.py:101
  383.2 4.5 collective-permute-done.10
  388.4 1.6 collective-permute-done.11
  390.7 2.5 fusion.116
  393.1 2.2 copy.818
  399.0 4.3 copy.783
  403.3 6.2 %reshape.244 = f32[3,3,3,2,2,256]{5,4,3,0,1,2:T(2,128)S(1)} reshape(f32[3,3,3,2,2,128,2]{6,5,4,3,0,1,2:T(8,128)} %copy.783) | data formatting | bytes 221184 | tf_op jit(solution)/shard_map/reshape | solution.py:42
  410.4 3.6 collective-permute-done.12
  414.4 3.2 collective-permute-done.13
  417.9 42.8 %psum.61 = f32[3]{0:T(128)S(1)} all-reduce(f32[3]{0:T(128)S(1)} %get-tuple-element.14), channel_id=1, replica_groups=mesh['old'=4,'new'=8] {'old','new'}, use_global_device_ids=true, to_apply=%region_17.18 | all-reduce | flops 3 | bytes 24 | tf_op jit(solution)/shard_map/psum | solution.py:154
  460.9 38.9 %psum.62 = f32[3]{0:T(128)S(1)} all-reduce(f32[3]{0:T(128)S(1)} %get-tuple-element.12), channel_id=1, replica_groups=mesh['old'=4,'new'=8] {'old','new'}, use_global_device_ids=true, to_apply=%region_19.20 | all-reduce | flops 3 | bytes 24 | tf_op jit(solution)/shard_map/psum | solution.py:101
  500.1 4.5 collective-permute-done.14
  505.0 1.6 collective-permute-done.15
  507.3 2.5 fusion.115
  509.8 2.2 copy.824
  515.6 4.3 copy.785
  519.9 6.2 %reshape.245 = f32[3,3,3,2,2,256]{5,4,3,0,1,2:T(2,128)S(1)} reshape(f32[3,3,3,2,2,128,2]{6,5,4,3,0,1,2:T(8,128)} %copy.785) | data formatting | bytes 221184 | tf_op jit(solution)/shard_map/reshape | solution.py:42
  527.1 3.6 collective-permute-done.16
  531.1 3.1 collective-permute-done.17
  534.5 42.8 %psum.63 = f32[3]{0:T(128)S(1)} all-reduce(f32[3]{0:T(128)S(1)} %get-tuple-element.10), channel_id=1, replica_groups=mesh['old'=4,'new'=8] {'old','new'}, use_global_device_ids=true, to_apply=%region_21.22 | all-reduce | flops 3 | bytes 24 | tf_op jit(solution)/shard_map/psum | solution.py:154
  577.3 0.8 multiply_subtract_fusion
  (333 shorter events, 34.3 us)
Async XLA Ops:
  10.8 18.5 %copy-start.2 = (bf16[4,27,125]{2,0,1:T(4,128)(2,1)S(1)}, bf16[4,27,125]{2,0,1:T(4,128)(2,1)}, u32[]{:S(2)}) copy-start(bf16[4,27,125]{2,0,1:T(4,128)(2,1)} %param.17) | copy-start | bytes 81004
  10.8 18.5 %copy-start.3 = (bf16[4,27,125]{2,0,1:T(4,128)(2,1)S(1)}, bf16[4,27,125]{2,0,1:T(4,128)(2,1)}, u32[]{:S(2)}) copy-start(bf16[4,27,125]{2,0,1:T(4,128)(2,1)} %param.18) | copy-start | bytes 81004
  12.3 11.8 %copy-start.5 = (s32[1024,1]{0,1:T(1,128)}, s32[1024,1]{0,1:T(1,128)S(1)}, u32[]{:S(2)}) copy-start(s32[1024,1]{0,1:T(1,128)S(1)} %compare_select_fusion.1) | copy-start | bytes 12292
  17.3 42.0 %all-to-all-start = ((s32[1,32,128]{2,0,1:T(1,128)}), s32[1,32,128]{2,0,1:T(1,128)S(1)}, u32[]{:S(2)}, u32[]{:S(2)}) async-start(s32[1,32,128]{2,0,1:T(1,128)} %bitcast.6), calls=%async_computation | async-start | bytes 32768 | tf_op jit(solution)/shard_map/all_to_all | solution.py:132
  48.2 3.6 copy-start
  59.3 37.9 %all-to-all-start.1 = ((f32[81,32,128]{2,0,1:T(8,128)}), f32[81,32,128]{2,0,1:T(8,128)S(1)}, u32[]{:S(2)}, u32[]{:S(2)}) async-start(f32[81,32,128]{2,0,1:T(8,128)} %copy.641), calls=%async_computation.1 | async-start | bytes 2883584 | tf_op jit(solution)/shard_map/all_to_all | solution.py:125
  139.4 3.7 collective-permute-start
  143.4 3.3 collective-permute-start.1
  147.0 4.6 collective-permute-start.2
  151.7 1.6 collective-permute-start.3
  158.8 1.5 copy-start.1
  159.6 2.4 copy-start.4
  173.8 3.7 collective-permute-start.4
  177.8 3.3 collective-permute-start.5
  266.1 4.6 collective-permute-start.6
  270.9 1.8 collective-permute-start.7
  293.1 3.7 collective-permute-start.8
  297.1 3.3 collective-permute-start.9
  383.2 4.6 collective-permute-start.10
  387.9 2.0 collective-permute-start.11
  410.3 3.7 collective-permute-start.12
  414.3 3.3 collective-permute-start.13
  500.0 4.6 collective-permute-start.14
  504.8 1.8 collective-permute-start.15
  526.9 3.7 collective-permute-start.16
  530.9 3.3 collective-permute-start.17
where the time goes:
time: 588 us; the launch traced here: 578 us
  blocking collectives  291 us (49%)
  local copies, waits for them, and re-layouts  109 us (19%)
  waiting for transfers between devices  85.1 us (14%)
  other arithmetic  59.1 us (10%)
  starting transfers between devices  17.8 us (3%)
  matrix products  13.5 us (2%)
    psum x4, blocking collectives, squares(): lax.psum(jnp.sum(residual * residual, axis=(1, 2, 3)), ('old', 'new'))  162 us
    psum x3, blocking collectives, on_device(): lax.psum(jnp.sum(direction * applied, axis=(1, 2, 3)), ('old', 'new'))  128 us
    ppermute x18, waiting for transfers between devices, passed_along(): lax.ppermute(shard, axis, [(i, (i + by) % size) for i in range(size)])  53.7 us
    reshape x20, local copies, waits for them, and re-layouts, merge_axis(): woven = woven.reshape(woven.shape[:-2] + (2 * count,))  52.6 us
    all_to_all x1, waiting for transfers between devices, on_device(): lax.all_to_all(outgoing.reshape(81, devices, capacity), ('old', 'new'), s...  31.4 us
    scatter-add x1, other arithmetic, on_device(): jnp.zeros((81, elements + 1), jnp.float32).at[:, slot_element].add(arrived)  28 us
    unnamed x39, local copies, waits for them, and re-layouts  16.9 us
  transfers between devices with their start and end apart: 20, of which 19 were waited for; matrix products, arithmetic and copies ran while one was open for 6% of the time, Pallas kernels for 0%

commit v1 on v0

--- a/solution.py
+++ b/solution.py
@@ -151,7 +151,7 @@
     norm_now = squares(residual)
     for iteration in range(ITERS):
         applied = operate(direction, volume)
-        curvature = lax.psum(jnp.sum(direction * applied, axis=(1, 2, 3)), ("old", "new"))
+        curvature = lax.psum(lax.psum(jnp.sum(direction * applied, axis=(1, 2, 3)), "old"), "new")
         step_size = norm_now / curvature
         solution = solution + step_size[:, None, None, None] * direction
         residual = residual - step_size[:, None, None, None] * applied

time: 588 us -> 566 us (0.963)
  the two profiles are of different devices: /device:TPU:10 before, /device:TPU:0 now
where the time goes in v1:
time: 566 us; the launch traced here: 557 us
  blocking collectives  250 us (44%)
  local copies, waits for them, and re-layouts  109 us (19%)
  waiting for transfers between devices  90.3 us (16%)
  other arithmetic  57.9 us (10%)
  starting transfers between devices  32.9 us (6%)
  matrix products  13.5 us (2%)
    psum x4, blocking collectives, squares(): lax.psum(jnp.sum(residual * residual, axis=(1, 2, 3)), ('old', 'new'))  153 us
    psum x4, blocking collectives, on_device(): lax.psum(lax.psum(jnp.sum(direction * applied, axis=(1, 2, 3)), 'old'), '...  74.1 us
    ppermute x18, waiting for transfers between devices, passed_along(): lax.ppermute(shard, axis, [(i, (i + by) % size) for i in range(size)])  55 us
    reshape x20, local copies, waits for them, and re-layouts, merge_axis(): woven = woven.reshape(woven.shape[:-2] + (2 * count,))  52.7 us
    all_to_all x1, waiting for transfers between devices, on_device(): lax.all_to_all(outgoing.reshape(81, devices, capacity), ('old', 'new'), s...  35.3 us
    scatter-add x1, other arithmetic, on_device(): jnp.zeros((81, elements + 1), jnp.float32).at[:, slot_element].add(arrived)  26.7 us
    psum x4, blocking collectives, on_device(): lax.psum(jnp.sum(direction * applied, axis=(1, 2, 3)), 'old')  22.9 us
    ppermute x18, starting transfers between devices, passed_along(): lax.ppermute(shard, axis, [(i, (i + by) % size) for i in range(size)])  19.8 us
  transfers between devices with their start and end apart: 20, of which 19 were waited for; matrix products, arithmetic and copies ran while one was open for 7% of the time, Pallas kernels for 0%

profile of v1, /device:TPU:0, one launch (start us, length us, event | category | flops | bytes accessed | tf_op | source)
XLA Modules:
  0.0 556.8 jit_solution(1704380572184772029)
XLA Ops:
  1.3 9.0 %reduce-window.6 = s32[32,8,128]{2,1,0:T(8,128)S(1)} reduce-window(s32[32,8,128]{2,1,0:T(8,128)S(1)} %fusion.60, s32[]{:T(128)} %constant.17.clone.1), window={size=1x1x128 pad=0_0x0_0x127_0}, to_apply=%region_0.0 | reduce-window | flops 4161536 | bytes 262148 | tf_op jit(solution)/shard_map/reduce-window
  12.3 5.1 scatter_custom_fusion
  17.3 7.3 %all-to-all-start = ((s32[1,32,128]{2,0,1:T(1,128)}), s32[1,32,128]{2,0,1:T(1,128)S(1)}, u32[]{:S(2)}, u32[]{:S(2)}) async-start(s32[1,32,128]{2,0,1:T(1,128)} %bitcast.6), calls=%async_computation | async-start | bytes 32768 | tf_op jit(solution)/shard_map/all_to_all | solution.py:132
  26.1 4.5 copy.623
  31.3 7.5 %gather_fusion = bf16[1024,3,27]{2,1,0:T(4,128)(2,1)} fusion(bf16[3,27,3072]{1,0,2:T(4,128)(2,1)S(1)} %copy.623, s32[1024]{0:T(1024)S(1)} %fusion.106), kind=kCustom, calls=%fused_computation | custom fusion | bytes 335872 | tf_op jit(solution)/shard_map/jit(_take)/gather | solution.py:116
  38.9 9.2 %select_bitcast_fusion.3 = (bf16[3,27,1024]{1,0,2:T(4,128)(2,1)}, bf16[3,27,1024]{1,0,2:T(4,128)(2,1)S(1)}, bf16[3,27,1024]{1,0,2:T(4,128)(2,1)S(1)}, bf16[3,27,1024]{1,0,2:T(4,128)(2,1)S(1)}) fusion(pred[1024]{0:T(1024)(128)(4,1)S(1)} %get-tuple-element.118, bf16[1024,3,27]{2,1,0:T(4,128)(2,1)} %gather_fusion, pred[1024]{0:T(1024)(128)(4,1)S(1)} %get-tuple-element.124, ...), kind=kLoop, calls=%fused_computation.31 | loop fusion | flops 414720 | bytes 834560 | tf_op jit(solution)/shard_map/jit(_where)/select_n | solution.py:88
  49.5 2.2 fusion.5
  53.1 1.7 fusion.11
  55.1 3.8 scatter_custom_fusion.1
  58.9 1.7 copy.641
  60.6 5.8 %all-to-all-start.1 = ((f32[81,32,128]{2,0,1:T(8,128)}), f32[81,32,128]{2,0,1:T(8,128)S(1)}, u32[]{:S(2)}, u32[]{:S(2)}) async-start(f32[81,32,128]{2,0,1:T(8,128)} %copy.641), calls=%async_computation.1 | async-start | bytes 2883584 | tf_op jit(solution)/shard_map/all_to_all | solution.py:125
  67.1 35.3 %all-to-all-done.1 = f32[81,32,128]{2,0,1:T(8,128)S(1)} async-done(((f32[81,32,128]{2,0,1:T(8,128)}), f32[81,32,128]{2,0,1:T(8,128)S(1)}, u32[]{:S(2)}, u32[]{:S(2)}) %all-to-all-start.1) | async-done | bytes 1327136 | tf_op jit(solution)/shard_map/all_to_all | solution.py:125
  104.6 26.7 %scatter_custom_fusion.2 = f32[81,513]{0,1:T(8,128)S(1)} fusion(s32[4096]{0:T(1024)} %bitcast.616, f32[4096,81]{1,0:T(8,128)S(1)} %copy.643, f32[]{:T(128)} %constant.14.clone.1), kind=kCustom, calls=%fused_computation.113 | custom fusion | flops 331776 | bytes 166724 | tf_op jit(solution)/shard_map/scatter-add | solution.py:143
  132.0 4.3 copy.777
  136.3 6.2 %reshape.241 = f32[3,3,3,2,2,256]{5,4,3,0,1,2:T(2,128)S(1)} reshape(f32[3,3,3,2,2,128,2]{6,5,4,3,0,1,2:T(8,128)} %copy.777) | data formatting | bytes 221184 | tf_op jit(solution)/shard_map/reshape | solution.py:42
  143.3 1.6 collective-permute-start
  145.0 4.7 collective-permute-done
  150.2 3.1 collective-permute-done.1
  153.6 3.6 collective-permute-done.2
  157.5 1.6 collective-permute-done.3
  159.8 2.5 fusion.118
  162.3 2.2 copy.806
  168.2 4.3 copy.779
  172.5 6.2 %reshape.242 = f32[3,3,3,2,2,256]{5,4,3,0,1,2:T(2,128)S(1)} reshape(f32[3,3,3,2,2,128,2]{6,5,4,3,0,1,2:T(8,128)} %copy.779) | data formatting | bytes 221184 | tf_op jit(solution)/shard_map/reshape | solution.py:42
  179.7 6.3 %collective-permute-done.4 = f32[3,5,5]{2,0,1:T(4,128)S(1)} collective-permute-done((f32[3,5,5]{2,0,1:T(4,128)S(1)}, f32[3,5,5]{2,0,1:T(4,128)S(1)}, u32[]{:S(2)}, u32[]{:S(2)}) %collective-permute-start.4) | collective-permute-done | bytes 332 | tf_op jit(solution)/shard_map/ppermute | solution.py:13
  186.3 3.2 collective-permute-done.5
  189.8 5.7 %psum.85 = f32[3]{0:T(128)S(1)} all-reduce(f32[3]{0:T(128)S(1)} %get-tuple-element.6), channel_id=1, replica_groups=mesh['old'=4,'new'=8] {'old'}, use_global_device_ids=true, to_apply=%region_9.10 | all-reduce | flops 3 | bytes 24 | tf_op jit(solution)/shard_map/psum | solution.py:154
  195.5 17.1 %psum.86 = f32[3]{0:T(128)S(1)} all-reduce(f32[3]{0:T(128)S(1)} %psum.85), channel_id=1, replica_groups=mesh['old'=4,'new'=8] {'new'}, use_global_device_ids=true, to_apply=%region_10.11 | all-reduce | flops 3 | bytes 24 | tf_op jit(solution)/shard_map/psum | solution.py:154
  212.6 37.4 %psum.84 = f32[3]{0:T(128)S(1)} all-reduce(f32[3]{0:T(128)S(1)} %get-tuple-element.7), channel_id=1, replica_groups=mesh['old'=4,'new'=8] {'old','new'}, use_global_device_ids=true, to_apply=%region_7.8 | all-reduce | flops 3 | bytes 24 | tf_op jit(solution)/shard_map/psum | solution.py:101
  250.2 42.1 %psum.87 = f32[3]{0:T(128)S(1)} all-reduce(f32[3]{0:T(128)S(1)} %get-tuple-element.18), channel_id=1, replica_groups=mesh['old'=4,'new'=8] {'old','new'}, use_global_device_ids=true, to_apply=%region_12.13 | all-reduce | flops 3 | bytes 24 | tf_op jit(solution)/shard_map/psum | solution.py:101
  292.6 3.3 collective-permute-start.6
  297.8 1.6 collective-permute-done.7
  300.0 2.5 fusion.117
  302.5 2.2 copy.812
  308.3 4.3 copy.781
  312.7 6.2 %reshape.243 = f32[3,3,3,2,2,256]{5,4,3,0,1,2:T(2,128)S(1)} reshape(f32[3,3,3,2,2,128,2]{6,5,4,3,0,1,2:T(8,128)} %copy.781) | data formatting | bytes 221184 | tf_op jit(solution)/shard_map/reshape | solution.py:42
  319.7 2.2 collective-permute-start.8
  322.0 4.3 collective-permute-done.8
  326.8 3.1 collective-permute-done.9
  330.2 5.6 %psum.88 = f32[3]{0:T(128)S(1)} all-reduce(f32[3]{0:T(128)S(1)} %get-tuple-element.16), channel_id=1, replica_groups=mesh['old'=4,'new'=8] {'old'}, use_global_device_ids=true, to_apply=%region_14.15 | all-reduce | flops 3 | bytes 24 | tf_op jit(solution)/shard_map/psum | solution.py:154
  335.9 19.1 %psum.89 = f32[3]{0:T(128)S(1)} all-reduce(f32[3]{0:T(128)S(1)} %psum.88), channel_id=1, replica_groups=mesh['old'=4,'new'=8] {'new'}, use_global_device_ids=true, to_apply=%region_15.16 | all-reduce | flops 3 | bytes 24 | tf_op jit(solution)/shard_map/psum | solution.py:154
  355.2 36.8 %psum.90 = f32[3]{0:T(128)S(1)} all-reduce(f32[3]{0:T(128)S(1)} %get-tuple-element.14), channel_id=1, replica_groups=mesh['old'=4,'new'=8] {'old','new'}, use_global_device_ids=true, to_apply=%region_17.18 | all-reduce | flops 3 | bytes 24 | tf_op jit(solution)/shard_map/psum | solution.py:101
  392.3 4.0 collective-permute-start.10
  398.3 1.6 collective-permute-done.11
  400.6 2.5 fusion.116
  403.0 2.2 copy.818
  408.9 4.3 copy.783
  413.2 6.2 %reshape.244 = f32[3,3,3,2,2,256]{5,4,3,0,1,2:T(2,128)S(1)} reshape(f32[3,3,3,2,2,128,2]{6,5,4,3,0,1,2:T(8,128)} %copy.783) | data formatting | bytes 221184 | tf_op jit(solution)/shard_map/reshape | solution.py:42
  420.2 1.5 collective-permute-start.12
  421.8 5.1 collective-permute-done.12
  427.4 3.1 collective-permute-done.13
  430.8 5.9 %psum.91 = f32[3]{0:T(128)S(1)} all-reduce(f32[3]{0:T(128)S(1)} %get-tuple-element.12), channel_id=1, replica_groups=mesh['old'=4,'new'=8] {'old'}, use_global_device_ids=true, to_apply=%region_19.20 | all-reduce | flops 3 | bytes 24 | tf_op jit(solution)/shard_map/psum | solution.py:154
  436.7 18.8 %psum.92 = f32[3]{0:T(128)S(1)} all-reduce(f32[3]{0:T(128)S(1)} %psum.91), channel_id=1, replica_groups=mesh['old'=4,'new'=8] {'new'}, use_global_device_ids=true, to_apply=%region_20.21 | all-reduce | flops 3 | bytes 24 | tf_op jit(solution)/shard_map/psum | solution.py:154
  455.7 36.8 %psum.93 = f32[3]{0:T(128)S(1)} all-reduce(f32[3]{0:T(128)S(1)} %get-tuple-element.10), channel_id=1, replica_groups=mesh['old'=4,'new'=8] {'old','new'}, use_global_device_ids=true, to_apply=%region_22.23 | all-reduce | flops 3 | bytes 24 | tf_op jit(solution)/shard_map/psum | solution.py:101
  492.8 4.0 collective-permute-start.14
  498.6 1.6 collective-permute-done.15
  500.9 2.5 fusion.115
  503.3 2.2 copy.824
  509.2 4.3 copy.785
  513.5 6.2 %reshape.245 = f32[3,3,3,2,2,256]{5,4,3,0,1,2:T(2,128)S(1)} reshape(f32[3,3,3,2,2,128,2]{6,5,4,3,0,1,2:T(8,128)} %copy.785) | data formatting | bytes 221184 | tf_op jit(solution)/shard_map/reshape | solution.py:42
  522.1 5.1 collective-permute-done.16
  527.7 3.1 collective-permute-done.17
  531.1 5.6 %psum.94 = f32[3]{0:T(128)S(1)} all-reduce(f32[3]{0:T(128)S(1)} %get-tuple-element.8), channel_id=1, replica_groups=mesh['old'=4,'new'=8] {'old'}, use_global_device_ids=true, to_apply=%region_24.25 | all-reduce | flops 3 | bytes 24 | tf_op jit(solution)/shard_map/psum | solution.py:154
  536.7 19.1 %psum.95 = f32[3]{0:T(128)S(1)} all-reduce(f32[3]{0:T(128)S(1)} %psum.94), channel_id=1, replica_groups=mesh['old'=4,'new'=8] {'new'}, use_global_device_ids=true, to_apply=%region_25.26 | all-reduce | flops 3 | bytes 24 | tf_op jit(solution)/shard_map/psum | solution.py:154
  (338 shorter events, 44.8 us)
Async XLA Ops:
  10.8 19.8 %copy-start.2 = (bf16[4,27,125]{2,0,1:T(4,128)(2,1)S(1)}, bf16[4,27,125]{2,0,1:T(4,128)(2,1)}, u32[]{:S(2)}) copy-start(bf16[4,27,125]{2,0,1:T(4,128)(2,1)} %param.17) | copy-start | bytes 81004
  10.8 19.8 %copy-start.3 = (bf16[4,27,125]{2,0,1:T(4,128)(2,1)S(1)}, bf16[4,27,125]{2,0,1:T(4,128)(2,1)}, u32[]{:S(2)}) copy-start(bf16[4,27,125]{2,0,1:T(4,128)(2,1)} %param.18) | copy-start | bytes 81004
  12.3 13.1 %copy-start.5 = (s32[1024,1]{0,1:T(1,128)}, s32[1024,1]{0,1:T(1,128)S(1)}, u32[]{:S(2)}) copy-start(s32[1024,1]{0,1:T(1,128)S(1)} %compare_select_fusion.1) | copy-start | bytes 12292
  17.3 43.3 %all-to-all-start = ((s32[1,32,128]{2,0,1:T(1,128)}), s32[1,32,128]{2,0,1:T(1,128)S(1)}, u32[]{:S(2)}, u32[]{:S(2)}) async-start(s32[1,32,128]{2,0,1:T(1,128)} %bitcast.6), calls=%async_computation | async-start | bytes 32768 | tf_op jit(solution)/shard_map/all_to_all | solution.py:132
  49.5 3.6 copy-start
  60.6 41.7 %all-to-all-start.1 = ((f32[81,32,128]{2,0,1:T(8,128)}), f32[81,32,128]{2,0,1:T(8,128)S(1)}, u32[]{:S(2)}, u32[]{:S(2)}) async-start(f32[81,32,128]{2,0,1:T(8,128)} %copy.641), calls=%async_computation.1 | async-start | bytes 2883584 | tf_op jit(solution)/shard_map/all_to_all | solution.py:125
  143.3 6.4 %collective-permute-start = (f32[3,5,5]{2,0,1:T(4,128)S(1)}, f32[3,5,5]{2,0,1:T(4,128)S(1)}, u32[]{:S(2)}, u32[]{:S(2)}) collective-permute-start(f32[3,5,5]{2,0,1:T(4,128)S(1)} %bitcast.617), channel_id=1, source_target_pairs={{0,1},{1,2},{2,3},{3,4},{4,5},{5,6},{6,7},{7,0},{8,9},{9,10},{10,1... | collective-permute-start | bytes 908 | tf_op jit(solution)/shard_map/ppermute | solution.py:13
  150.0 3.3 collective-permute-start.1
  153.6 3.7 collective-permute-start.2
  157.5 1.6 collective-permute-start.3
  164.5 1.5 copy-start.1
  165.3 2.4 copy-start.4
  179.5 6.4 %collective-permute-start.4 = (f32[3,5,5]{2,0,1:T(4,128)S(1)}, f32[3,5,5]{2,0,1:T(4,128)S(1)}, u32[]{:S(2)}, u32[]{:S(2)}) collective-permute-start(f32[3,5,5]{2,0,1:T(4,128)S(1)} %bitcast.619), channel_id=1, source_target_pairs={{0,1},{1,2},{2,3},{3,4},{4,5},{5,6},{6,7},{7,0},{8,9},{9,10},{10,1... | collective-permute-start | bytes 908 | tf_op jit(solution)/shard_map/ppermute | solution.py:13
  186.3 3.3 collective-permute-start.5
  292.6 4.6 collective-permute-start.6
  297.5 1.8 collective-permute-start.7
  319.7 6.6 %collective-permute-start.8 = (f32[3,5,5]{2,0,1:T(4,128)S(1)}, f32[3,5,5]{2,0,1:T(4,128)S(1)}, u32[]{:S(2)}, u32[]{:S(2)}) collective-permute-start(f32[3,5,5]{2,0,1:T(4,128)S(1)} %bitcast.621), channel_id=1, source_target_pairs={{0,1},{1,2},{2,3},{3,4},{4,5},{5,6},{6,7},{7,0},{8,9},{9,10},{10,1... | collective-permute-start | bytes 908 | tf_op jit(solution)/shard_map/ppermute | solution.py:13
  326.7 3.3 collective-permute-start.9
  392.3 5.4 collective-permute-start.10
  397.8 2.0 collective-permute-start.11
  420.2 6.7 %collective-permute-start.12 = (f32[3,5,5]{2,0,1:T(4,128)S(1)}, f32[3,5,5]{2,0,1:T(4,128)S(1)}, u32[]{:S(2)}, u32[]{:S(2)}) collective-permute-start(f32[3,5,5]{2,0,1:T(4,128)S(1)} %bitcast.623), channel_id=1, source_target_pairs={{0,1},{1,2},{2,3},{3,4},{4,5},{5,6},{6,7},{7,0},{8,9},{9,10},{10,1... | collective-permute-start | bytes 908 | tf_op jit(solution)/shard_map/ppermute | solution.py:13
  427.2 3.3 collective-permute-start.13
  492.8 5.4 collective-permute-start.14
  498.4 1.8 collective-permute-start.15
  520.5 6.7 %collective-permute-start.16 = (f32[3,5,5]{2,0,1:T(4,128)S(1)}, f32[3,5,5]{2,0,1:T(4,128)S(1)}, u32[]{:S(2)}, u32[]{:S(2)}) collective-permute-start(f32[3,5,5]{2,0,1:T(4,128)S(1)} %bitcast.625), channel_id=1, source_target_pairs={{0,1},{1,2},{2,3},{3,4},{4,5},{5,6},{6,7},{7,0},{8,9},{9,10},{10,1... | collective-permute-start | bytes 908 | tf_op jit(solution)/shard_map/ppermute | solution.py:13
  527.5 3.3 collective-permute-start.17
